TPU v7x, 1024 devices: a whole 4x8x16 slice. The times are simulated.
1024 devices in a mesh: seq: 128 (over y, z), head: 8 (over x, core).
Axes of the slice: x: 4, y: 8, z: 16, core: 2. Of those that a mesh axis runs over, the one named last changes fastest.
Arguments:
- query_rows: bfloat16 [16384, 4096], P('seq', 'head'), may hold values from -6 to 6
- key_rows: bfloat16 [16384, 4096], P('seq', 'head'), may hold values from -6 to 6
- value_rows: bfloat16 [16384, 4096], P('seq', 'head'), may hold values from -70 to 70
- log_decay: float32 [32, 16384], P('head', 'seq'), may hold values from -1.6 to 0
- cotangent: bfloat16 [16384, 4096], P('seq', 'head'), may hold values from -6 to 6
Outputs:
- attended: bfloat16 [16384, 4096], P('seq', 'head')
- query_grad: bfloat16 [16384, 4096], P('seq', 'head')
- key_grad: bfloat16 [16384, 4096], P('seq', 'head')
- value_grad: bfloat16 [16384, 4096], P('seq', 'head')
All inputs are finite; a program needn't handle non-finite values.
Results may differ from a plain program's by a relative error of at most 0.0054.
Values sent between devices are 32-bit elements; how exact they have to be, the bound alone decides.
A program may use at most 128 MiB of HBM per device.

v0:
```python
import jax
import jax.numpy as jnp
from jax import lax
from jax.sharding import PartitionSpec as P

highest = lax.Precision.HIGHEST


def passed_along(block, axis, distance):
    devices = range(lax.axis_size(axis))
    route = [(i - distance, i) for i in devices if i - distance in devices]
    return lax.ppermute(block, axis, route)


def combine(earlier, later):
    return (earlier[0] + later[0], jnp.exp(later[0])[:, None, None] * earlier[1] + later[1])


def hop_list(length):
    hops = [1]
    stride = 1
    while stride < length:
        hops.append(stride)
        stride = stride * 2
    return hops


def forward_chain(pair):
    current = pair
    for number, stride in enumerate(hop_list(lax.axis_size("seq"))):
        moved = passed_along((current[0], current[1]), "seq", stride)
        current = moved if number == 0 else combine(moved, current)
    return current


def backward_chain(pair):
    current = pair
    for number, stride in enumerate(hop_list(lax.axis_size("seq"))):
        moved = passed_along((current[0], current[1]), "seq", -stride)
        current = moved if number == 0 else combine(moved, current)
    return current


def local(query_rows, key_rows, value_rows, log_decay, cotangent):
    head_count, row_count = log_decay.shape
    head_size = query_rows.shape[1] // head_count
    full_width = head_size * head_count * lax.axis_size("head")

    def split_heads(matrix):
        return matrix.reshape(row_count, head_count, head_size).transpose(1, 0, 2)

    def join_heads(stack):
        return stack.transpose(1, 0, 2).reshape(row_count, head_count * head_size)

    query_heads = split_heads(query_rows)
    key_heads = split_heads(key_rows)
    value_heads = split_heads(value_rows)
    cumulative = jnp.cumsum(log_decay, axis=1)
    totals = cumulative[:, -1]
    fade_out = jnp.exp(totals[:, None] - cumulative)[..., None]
    growth = jnp.exp(cumulative)[..., None]
    element_indices = lax.iota(jnp.int32, row_count)
    causal = element_indices[:, None] >= element_indices[None, :]

    def weights_of(query_one, key_one, running):
        spread = running[:, None] - running[None, :]
        decay_matrix = jnp.where(causal, jnp.exp(jnp.minimum(spread, 0.0)), 0.0)
        scores = jnp.einsum("td,sd->ts", query_one, key_one, preferred_element_type=jnp.float32)
        return ((scores * decay_matrix).astype(jnp.bfloat16), decay_matrix)

    def forward_head(inputs):
        query_one, key_one, value_one, running = inputs
        weights, _ = weights_of(query_one, key_one, running)
        return jnp.dot(weights, value_one, preferred_element_type=jnp.float32)

    scaled_keys = (key_heads.astype(jnp.float32) * fade_out).astype(jnp.bfloat16)
    local_state = jnp.einsum(
        "htd,hte->hde", scaled_keys, value_heads, preferred_element_type=jnp.float32
    )
    state_in = forward_chain((totals, local_state))[1]
    intra = lax.map(forward_head, (query_heads, key_heads, value_heads, cumulative))
    scaled_queries = query_heads.astype(jnp.float32) * growth
    raw = join_heads(
        jnp.einsum("htd,hde->hte", scaled_queries, state_in, precision=highest) + intra
    )
    square_sum = lax.psum(jnp.sum(raw * raw, axis=1), "head")
    inverse_norm = lax.rsqrt(square_sum / full_width + 1e-06)[:, None]
    normed = raw * inverse_norm
    attended = normed.astype(jnp.bfloat16)
    upstream = cotangent.astype(jnp.float32)
    dot_sum = lax.psum(jnp.sum(upstream * normed, axis=1), "head")
    raw_grad = (inverse_norm * (upstream - normed * (dot_sum / full_width)[:, None])).astype(
        jnp.bfloat16
    )
    grad_heads = split_heads(raw_grad)
    grad_float = grad_heads.astype(jnp.float32)
    query_state = jnp.einsum("htd,hte->hde", scaled_queries, grad_float, precision=highest)
    grad_state = backward_chain((totals, query_state))[1]

    def backward_head(inputs):
        query_one, key_one, value_one, grad_one, running = inputs
        weights, decay_matrix = weights_of(query_one, key_one, running)
        grad_scores = jnp.einsum(
            "te,se->ts", grad_one, value_one, preferred_element_type=jnp.float32
        )
        grad_weights = (grad_scores * decay_matrix).astype(jnp.bfloat16)
        query_part = jnp.dot(grad_weights, key_one, preferred_element_type=jnp.float32)
        key_part = jnp.einsum(
            "ts,td->sd", grad_weights, query_one, preferred_element_type=jnp.float32
        )
        value_part = jnp.einsum("ts,te->se", weights, grad_one, preferred_element_type=jnp.float32)
        return (query_part, key_part, value_part)

    pieces = lax.map(backward_head, (query_heads, key_heads, value_heads, grad_heads, cumulative))
    query_total = (
        growth * jnp.einsum("hte,hde->htd", grad_float, state_in, precision=highest) + pieces[0]
    )
    key_total = pieces[1] + fade_out * jnp.einsum(
        "hse,hde->hsd", value_heads.astype(jnp.float32), grad_state, precision=highest
    )
    value_total = pieces[2] + fade_out * jnp.einsum(
        "hsd,hde->hse", key_heads.astype(jnp.float32), grad_state, precision=highest
    )
    query_grad = join_heads(query_total).astype(jnp.bfloat16)
    key_grad = join_heads(key_total).astype(jnp.bfloat16)
    value_grad = join_heads(value_total).astype(jnp.bfloat16)
    return (attended, query_grad, key_grad, value_grad)


def solution(mesh):
    return jax.shard_map(
        local,
        mesh=mesh,
        in_specs=(
            P("seq", "head"),
            P("seq", "head"),
            P("seq", "head"),
            P("head", "seq"),
            P("seq", "head"),
        ),
        out_specs=(P("seq", "head"), P("seq", "head"), P("seq", "head"), P("seq", "head")),
        check_vma=False,
    )
```

profile of v0, /device:TPU:81, one launch (start us, length us, event | category | flops | bytes accessed | tf_op | source)
XLA Modules:
  0.0 365.7 jit_solution(6432727743975345767)
XLA Ops:
  7.2 5.1 %collective-permute-done.7 = f32[4,128,128]{2,1,0:T(8,128)S(1)} collective-permute-done((f32[4,128,128]{2,1,0:T(8,128)S(1)}, f32[4,128,128]{2,1,0:T(8,128)S(1)}, u32[]{:S(2)}, u32[]{:S(2)}) %collective-permute-start.7) | collective-permute-done | bytes 262176 | tf_op jit(solution)/shard_map/ppermute | solution.py:12
  16.3 5.1 %collective-permute-start = (f32[4]{0:T(128)S(1)}, f32[4]{0:T(128)S(1)}, u32[]{:S(2)}, u32[]{:S(2)}) collective-permute-start(f32[4]{0:T(128)S(1)} %slice_reduce_fusion), channel_id=1, source_target_pairs={{0,8},{8,16},{16,24},{24,32},{32,40},{40,48},{48,56},{56,64},{64,7... | collective-permute-start | bytes 56 | tf_op jit(solution)/shard_map/ppermute | solution.py:12
  21.4 12.4 %collective-permute-done = f32[4]{0:T(128)S(1)} collective-permute-done((f32[4]{0:T(128)S(1)}, f32[4]{0:T(128)S(1)}, u32[]{:S(2)}, u32[]{:S(2)}) %collective-permute-start) | collective-permute-done | bytes 48 | tf_op jit(solution)/shard_map/ppermute | solution.py:12
  41.9 8.3 %collective-permute-done.9 = f32[4,128,128]{2,1,0:T(8,128)S(1)} collective-permute-done((f32[4,128,128]{2,1,0:T(8,128)S(1)}, f32[4,128,128]{2,1,0:T(8,128)S(1)}, u32[]{:S(2)}, u32[]{:S(2)}) %collective-permute-start.9) | collective-permute-done | bytes 262176 | tf_op jit(solution)/shard_map/ppermute | solution.py:12
  50.3 4.6 %collective-permute-start.10 = (f32[4,128,128]{2,1,0:T(8,128)S(1)}, f32[4,128,128]{2,1,0:T(8,128)S(1)}, u32[]{:S(2)}, u32[]{:S(2)}) collective-permute-start(f32[4,128,128]{2,1,0:T(8,128)S(1)} %multiply_add_fusion.12), channel_id=1, source_target_pairs={{0,32},{8,40},{16,48},{24,56},{32,64},{40,72},{48,80},{56,88},{64,... | collective-permute-start | bytes 786440 | tf_op jit(solution)/shard_map/ppermute | solution.py:12
  54.9 5.8 %collective-permute-start.2 = (f32[4]{0:T(128)S(1)}, f32[4]{0:T(128)S(1)}, u32[]{:S(2)}, u32[]{:S(2)}) collective-permute-start(f32[4]{0:T(128)S(1)} %get-tuple-element.220), channel_id=1, source_target_pairs={{0,16},{8,24},{16,32},{24,40},{32,48},{40,56},{48,64},{56,72},{64,... | collective-permute-start | bytes 56 | tf_op jit(solution)/shard_map/ppermute | solution.py:12
  60.7 12.3 %collective-permute-done.2 = f32[4]{0:T(128)S(1)} collective-permute-done((f32[4]{0:T(128)S(1)}, f32[4]{0:T(128)S(1)}, u32[]{:S(2)}, u32[]{:S(2)}) %collective-permute-start.2) | collective-permute-done | bytes 48 | tf_op jit(solution)/shard_map/ppermute | solution.py:12
  73.1 8.4 %collective-permute-start.11 = (f32[4,128,128]{2,1,0:T(8,128)S(1)}, f32[4,128,128]{2,1,0:T(8,128)S(1)}, u32[]{:S(2)}, u32[]{:S(2)}) collective-permute-start(f32[4,128,128]{2,1,0:T(8,128)S(1)} %multiply_add_fusion.11), channel_id=1, source_target_pairs={{0,64},{8,72},{16,80},{24,88},{32,96},{40,104},{48,112},{56,120},{... | collective-permute-start | bytes 786440 | tf_op jit(solution)/shard_map/ppermute | solution.py:12
  81.5 5.2 %collective-permute-start.3 = (f32[4]{0:T(128)S(1)}, f32[4]{0:T(128)S(1)}, u32[]{:S(2)}, u32[]{:S(2)}) collective-permute-start(f32[4]{0:T(128)S(1)} %get-tuple-element.218), channel_id=1, source_target_pairs={{0,32},{8,40},{16,48},{24,56},{32,64},{40,72},{48,80},{56,88},{64,... | collective-permute-start | bytes 56 | tf_op jit(solution)/shard_map/ppermute | solution.py:12
  90.9 8.0 %collective-permute-done.11 = f32[4,128,128]{2,1,0:T(8,128)S(1)} collective-permute-done((f32[4,128,128]{2,1,0:T(8,128)S(1)}, f32[4,128,128]{2,1,0:T(8,128)S(1)}, u32[]{:S(2)}, u32[]{:S(2)}) %collective-permute-start.11) | collective-permute-done | bytes 262176 | tf_op jit(solution)/shard_map/ppermute | solution.py:12
  99.0 4.9 %collective-permute-start.12 = (f32[4,128,128]{2,1,0:T(8,128)S(1)}, f32[4,128,128]{2,1,0:T(8,128)S(1)}, u32[]{:S(2)}, u32[]{:S(2)}) collective-permute-start(f32[4,128,128]{2,1,0:T(8,128)S(1)} %multiply_add_fusion.10), channel_id=1, source_target_pairs={{0,128},{8,136},{16,144},{24,152},{32,160},{40,168},{48,176},{56,1... | collective-permute-start | bytes 786440 | tf_op jit(solution)/shard_map/ppermute | solution.py:12
  103.9 7.6 %collective-permute-start.4 = (f32[4]{0:T(128)S(1)}, f32[4]{0:T(128)S(1)}, u32[]{:S(2)}, u32[]{:S(2)}) collective-permute-start(f32[4]{0:T(128)S(1)} %get-tuple-element.216), channel_id=1, source_target_pairs={{0,64},{8,72},{16,80},{24,88},{32,96},{40,104},{48,112},{56,120},{... | collective-permute-start | bytes 56 | tf_op jit(solution)/shard_map/ppermute | solution.py:12
  111.5 6.3 %collective-permute-done.4 = f32[4]{0:T(128)S(1)} collective-permute-done((f32[4]{0:T(128)S(1)}, f32[4]{0:T(128)S(1)}, u32[]{:S(2)}, u32[]{:S(2)}) %collective-permute-start.4) | collective-permute-done | bytes 48 | tf_op jit(solution)/shard_map/ppermute | solution.py:12
  117.9 5.6 %collective-permute-done.12 = f32[4,128,128]{2,1,0:T(8,128)S(1)} collective-permute-done((f32[4,128,128]{2,1,0:T(8,128)S(1)}, f32[4,128,128]{2,1,0:T(8,128)S(1)}, u32[]{:S(2)}, u32[]{:S(2)}) %collective-permute-start.12) | collective-permute-done | bytes 262176 | tf_op jit(solution)/shard_map/ppermute | solution.py:12
  129.5 9.0 %collective-permute-done.5 = f32[4]{0:T(128)S(1)} collective-permute-done((f32[4]{0:T(128)S(1)}, f32[4]{0:T(128)S(1)}, u32[]{:S(2)}, u32[]{:S(2)}) %collective-permute-start.5) | collective-permute-done | bytes 48 | tf_op jit(solution)/shard_map/ppermute | solution.py:12
  149.4 20.3 %psum.14 = f32[128]{0:T(128)S(1)} all-reduce(f32[128]{0:T(128)S(1)} %get-tuple-element.227), channel_id=1, replica_groups=mesh['seq'=128,'head'=8] {'head'}, use_global_device_ids=true, to_apply=%region_4.5 | all-reduce | flops 128 | bytes 1024 | tf_op jit(solution)/shard_map/psum | solution.py:86
  169.8 12.4 %psum.15 = f32[128]{0:T(128)S(1)} all-reduce(f32[128]{0:T(128)S(1)} %fusion.68), channel_id=1, replica_groups=mesh['seq'=128,'head'=8] {'head'}, use_global_device_ids=true, to_apply=%region_6.7 | all-reduce | flops 128 | bytes 1024 | tf_op jit(solution)/shard_map/psum | solution.py:91
  183.3 23.7 %collective-permute-start.22 = (f32[4,128,128]{2,1,0:T(8,128)S(1)}, f32[4,128,128]{2,1,0:T(8,128)S(1)}, u32[]{:S(2)}, u32[]{:S(2)}) collective-permute-start(f32[4,128,128]{2,1,0:T(8,128)S(1)} %fusion.72), channel_id=1, source_target_pairs={{8,0},{16,8},{24,16},{32,24},{40,32},{48,40},{56,48},{64,56},{72,6... | collective-permute-start | bytes 786440 | tf_op jit(solution)/shard_map/ppermute | solution.py:12
  207.0 5.0 %collective-permute-done.22 = f32[4,128,128]{2,1,0:T(8,128)S(1)} collective-permute-done((f32[4,128,128]{2,1,0:T(8,128)S(1)}, f32[4,128,128]{2,1,0:T(8,128)S(1)}, u32[]{:S(2)}, u32[]{:S(2)}) %collective-permute-start.22) | collective-permute-done | bytes 262176 | tf_op jit(solution)/shard_map/ppermute | solution.py:12
  225.8 9.6 %collective-permute-start.24 = (f32[4,128,128]{2,1,0:T(8,128)S(1)}, f32[4,128,128]{2,1,0:T(8,128)S(1)}, u32[]{:S(2)}, u32[]{:S(2)}) collective-permute-start(f32[4,128,128]{2,1,0:T(8,128)S(1)} %multiply_add_fusion.6), channel_id=1, source_target_pairs={{16,0},{24,8},{32,16},{40,24},{48,32},{56,40},{64,48},{72,56},{80,... | collective-permute-start | bytes 786440 | tf_op jit(solution)/shard_map/ppermute | solution.py:12
  235.4 7.7 %collective-permute-done.24 = f32[4,128,128]{2,1,0:T(8,128)S(1)} collective-permute-done((f32[4,128,128]{2,1,0:T(8,128)S(1)}, f32[4,128,128]{2,1,0:T(8,128)S(1)}, u32[]{:S(2)}, u32[]{:S(2)}) %collective-permute-start.24) | collective-permute-done | bytes 262176 | tf_op jit(solution)/shard_map/ppermute | solution.py:12
  243.1 8.1 %collective-permute-start.25 = (f32[4,128,128]{2,1,0:T(8,128)S(1)}, f32[4,128,128]{2,1,0:T(8,128)S(1)}, u32[]{:S(2)}, u32[]{:S(2)}) collective-permute-start(f32[4,128,128]{2,1,0:T(8,128)S(1)} %multiply_add_fusion.5), channel_id=1, source_target_pairs={{32,0},{40,8},{48,16},{56,24},{64,32},{72,40},{80,48},{88,56},{96,... | collective-permute-start | bytes 786440 | tf_op jit(solution)/shard_map/ppermute | solution.py:12
  253.2 16.4 %collective-permute-done.17 = f32[4]{0:T(128)S(1)} collective-permute-done((f32[4]{0:T(128)S(1)}, f32[4]{0:T(128)S(1)}, u32[]{:S(2)}, u32[]{:S(2)}) %collective-permute-start.17) | collective-permute-done | bytes 48 | tf_op jit(solution)/shard_map/ppermute | solution.py:12
  271.6 4.8 %collective-permute-start.18 = (f32[4]{0:T(128)S(1)}, f32[4]{0:T(128)S(1)}, u32[]{:S(2)}, u32[]{:S(2)}) collective-permute-start(f32[4]{0:T(128)S(1)} %get-tuple-element.208), channel_id=1, source_target_pairs={{32,0},{40,8},{48,16},{56,24},{64,32},{72,40},{80,48},{88,56},{96,... | collective-permute-start | bytes 56 | tf_op jit(solution)/shard_map/ppermute | solution.py:12
  276.4 11.1 %collective-permute-done.18 = f32[4]{0:T(128)S(1)} collective-permute-done((f32[4]{0:T(128)S(1)}, f32[4]{0:T(128)S(1)}, u32[]{:S(2)}, u32[]{:S(2)}) %collective-permute-start.18) | collective-permute-done | bytes 48 | tf_op jit(solution)/shard_map/ppermute | solution.py:12
  287.5 8.7 %collective-permute-done.26 = f32[4,128,128]{2,1,0:T(8,128)S(1)} collective-permute-done((f32[4,128,128]{2,1,0:T(8,128)S(1)}, f32[4,128,128]{2,1,0:T(8,128)S(1)}, u32[]{:S(2)}, u32[]{:S(2)}) %collective-permute-start.26) | collective-permute-done | bytes 262176 | tf_op jit(solution)/shard_map/ppermute | solution.py:12
  298.3 5.1 %collective-permute-start.19 = (f32[4]{0:T(128)S(1)}, f32[4]{0:T(128)S(1)}, u32[]{:S(2)}, u32[]{:S(2)}) collective-permute-start(f32[4]{0:T(128)S(1)} %get-tuple-element.206), channel_id=1, source_target_pairs={{64,0},{72,8},{80,16},{88,24},{96,32},{104,40},{112,48},{120,56},{... | collective-permute-start | bytes 56 | tf_op jit(solution)/shard_map/ppermute | solution.py:12
  303.4 7.9 %collective-permute-done.19 = f32[4]{0:T(128)S(1)} collective-permute-done((f32[4]{0:T(128)S(1)}, f32[4]{0:T(128)S(1)}, u32[]{:S(2)}, u32[]{:S(2)}) %collective-permute-start.19) | collective-permute-done | bytes 48 | tf_op jit(solution)/shard_map/ppermute | solution.py:12
  313.2 7.7 %collective-permute-done.27 = f32[4,128,128]{2,1,0:T(8,128)S(1)} collective-permute-done((f32[4,128,128]{2,1,0:T(8,128)S(1)}, f32[4,128,128]{2,1,0:T(8,128)S(1)}, u32[]{:S(2)}, u32[]{:S(2)}) %collective-permute-start.27) | collective-permute-done | bytes 262176 | tf_op jit(solution)/shard_map/ppermute | solution.py:12
  322.9 7.7 %collective-permute-done.20 = f32[4]{0:T(128)S(1)} collective-permute-done((f32[4]{0:T(128)S(1)}, f32[4]{0:T(128)S(1)}, u32[]{:S(2)}, u32[]{:S(2)}) %collective-permute-start.20) | collective-permute-done | bytes 48 | tf_op jit(solution)/shard_map/ppermute | solution.py:12
  332.5 12.8 %collective-permute-done.21 = f32[4]{0:T(128)S(1)} collective-permute-done((f32[4]{0:T(128)S(1)}, f32[4]{0:T(128)S(1)}, u32[]{:S(2)}, u32[]{:S(2)}) %collective-permute-start.21) | collective-permute-done | bytes 48 | tf_op jit(solution)/shard_map/ppermute | solution.py:12
  351.8 11.5 %collective-permute-done.29 = f32[4,128,128]{2,1,0:T(8,128)S(1)} collective-permute-done((f32[4,128,128]{2,1,0:T(8,128)S(1)}, f32[4,128,128]{2,1,0:T(8,128)S(1)}, u32[]{:S(2)}, u32[]{:S(2)}) %collective-permute-start.29) | collective-permute-done | bytes 262176 | tf_op jit(solution)/shard_map/ppermute | solution.py:12
  (120 shorter events, 80.6 us)
Async XLA Ops:
  0.6 1.1 copy-start.1
  3.2 9.1 %collective-permute-start.7 = (f32[4,128,128]{2,1,0:T(8,128)S(1)}, f32[4,128,128]{2,1,0:T(8,128)S(1)}, u32[]{:S(2)}, u32[]{:S(2)}) collective-permute-start(f32[4,128,128]{2,1,0:T(8,128)S(1)} %fusion.73), channel_id=1, source_target_pairs={{0,8},{8,16},{16,24},{24,32},{32,40},{40,48},{48,56},{56,64},{64,7... | collective-permute-start | bytes 786440 | tf_op jit(solution)/shard_map/ppermute | solution.py:12
  12.3 27.6 %collective-permute-start.8 = (f32[4,128,128]{2,1,0:T(8,128)S(1)}, f32[4,128,128]{2,1,0:T(8,128)S(1)}, u32[]{:S(2)}, u32[]{:S(2)}) collective-permute-start(f32[4,128,128]{2,1,0:T(8,128)S(1)} %collective-permute-done.7), channel_id=1, source_target_pairs={{0,8},{8,16},{16,24},{24,32},{32,40},{40,48},{48,56},{56,64},{64,7... | collective-permute-start | bytes 786440 | tf_op jit(solution)/shard_map/ppermute | solution.py:12
  16.3 17.5 %collective-permute-start = (f32[4]{0:T(128)S(1)}, f32[4]{0:T(128)S(1)}, u32[]{:S(2)}, u32[]{:S(2)}) collective-permute-start(f32[4]{0:T(128)S(1)} %slice_reduce_fusion), channel_id=1, source_target_pairs={{0,8},{8,16},{16,24},{24,32},{32,40},{40,48},{48,56},{56,64},{64,7... | collective-permute-start | bytes 56 | tf_op jit(solution)/shard_map/ppermute | solution.py:12
  33.7 6.1 %collective-permute-start.1 = (f32[4]{0:T(128)S(1)}, f32[4]{0:T(128)S(1)}, u32[]{:S(2)}, u32[]{:S(2)}) collective-permute-start(f32[4]{0:T(128)S(1)} %collective-permute-done), channel_id=1, source_target_pairs={{0,8},{8,16},{16,24},{24,32},{32,40},{40,48},{48,56},{56,64},{64,7... | collective-permute-start | bytes 56 | tf_op jit(solution)/shard_map/ppermute | solution.py:12
  40.0 10.2 %collective-permute-start.9 = (f32[4,128,128]{2,1,0:T(8,128)S(1)}, f32[4,128,128]{2,1,0:T(8,128)S(1)}, u32[]{:S(2)}, u32[]{:S(2)}) collective-permute-start(f32[4,128,128]{2,1,0:T(8,128)S(1)} %multiply_add_fusion.13), channel_id=1, source_target_pairs={{0,16},{8,24},{16,32},{24,40},{32,48},{40,56},{48,64},{56,72},{64,... | collective-permute-start | bytes 786440 | tf_op jit(solution)/shard_map/ppermute | solution.py:12
  50.3 22.7 %collective-permute-start.10 = (f32[4,128,128]{2,1,0:T(8,128)S(1)}, f32[4,128,128]{2,1,0:T(8,128)S(1)}, u32[]{:S(2)}, u32[]{:S(2)}) collective-permute-start(f32[4,128,128]{2,1,0:T(8,128)S(1)} %multiply_add_fusion.12), channel_id=1, source_target_pairs={{0,32},{8,40},{16,48},{24,56},{32,64},{40,72},{48,80},{56,88},{64,... | collective-permute-start | bytes 786440 | tf_op jit(solution)/shard_map/ppermute | solution.py:12
  54.9 18.1 %collective-permute-start.2 = (f32[4]{0:T(128)S(1)}, f32[4]{0:T(128)S(1)}, u32[]{:S(2)}, u32[]{:S(2)}) collective-permute-start(f32[4]{0:T(128)S(1)} %get-tuple-element.220), channel_id=1, source_target_pairs={{0,16},{8,24},{16,32},{24,40},{32,48},{40,56},{48,64},{56,72},{64,... | collective-permute-start | bytes 56 | tf_op jit(solution)/shard_map/ppermute | solution.py:12
  73.1 25.8 %collective-permute-start.11 = (f32[4,128,128]{2,1,0:T(8,128)S(1)}, f32[4,128,128]{2,1,0:T(8,128)S(1)}, u32[]{:S(2)}, u32[]{:S(2)}) collective-permute-start(f32[4,128,128]{2,1,0:T(8,128)S(1)} %multiply_add_fusion.11), channel_id=1, source_target_pairs={{0,64},{8,72},{16,80},{24,88},{32,96},{40,104},{48,112},{56,120},{... | collective-permute-start | bytes 786440 | tf_op jit(solution)/shard_map/ppermute | solution.py:12
  81.5 9.4 %collective-permute-start.3 = (f32[4]{0:T(128)S(1)}, f32[4]{0:T(128)S(1)}, u32[]{:S(2)}, u32[]{:S(2)}) collective-permute-start(f32[4]{0:T(128)S(1)} %get-tuple-element.218), channel_id=1, source_target_pairs={{0,32},{8,40},{16,48},{24,56},{32,64},{40,72},{48,80},{56,88},{64,... | collective-permute-start | bytes 56 | tf_op jit(solution)/shard_map/ppermute | solution.py:12
  99.0 24.4 %collective-permute-start.12 = (f32[4,128,128]{2,1,0:T(8,128)S(1)}, f32[4,128,128]{2,1,0:T(8,128)S(1)}, u32[]{:S(2)}, u32[]{:S(2)}) collective-permute-start(f32[4,128,128]{2,1,0:T(8,128)S(1)} %multiply_add_fusion.10), channel_id=1, source_target_pairs={{0,128},{8,136},{16,144},{24,152},{32,160},{40,168},{48,176},{56,1... | collective-permute-start | bytes 786440 | tf_op jit(solution)/shard_map/ppermute | solution.py:12
  103.9 13.9 %collective-permute-start.4 = (f32[4]{0:T(128)S(1)}, f32[4]{0:T(128)S(1)}, u32[]{:S(2)}, u32[]{:S(2)}) collective-permute-start(f32[4]{0:T(128)S(1)} %get-tuple-element.216), channel_id=1, source_target_pairs={{0,64},{8,72},{16,80},{24,88},{32,96},{40,104},{48,112},{56,120},{... | collective-permute-start | bytes 56 | tf_op jit(solution)/shard_map/ppermute | solution.py:12
  123.5 14.9 %collective-permute-start.13 = (f32[4,128,128]{2,1,0:T(8,128)S(1)}, f32[4,128,128]{2,1,0:T(8,128)S(1)}, u32[]{:S(2)}, u32[]{:S(2)}) collective-permute-start(f32[4,128,128]{2,1,0:T(8,128)S(1)} %multiply_add_fusion.9), channel_id=1, source_target_pairs={{0,256},{8,264},{16,272},{24,280},{32,288},{40,296},{48,304},{56,3... | collective-permute-start | bytes 786440 | tf_op jit(solution)/shard_map/ppermute | solution.py:12
  127.5 10.9 %collective-permute-start.5 = (f32[4]{0:T(128)S(1)}, f32[4]{0:T(128)S(1)}, u32[]{:S(2)}, u32[]{:S(2)}) collective-permute-start(f32[4]{0:T(128)S(1)} %get-tuple-element.214), channel_id=1, source_target_pairs={{0,128},{8,136},{16,144},{24,152},{32,160},{40,168},{48,176},{56,1... | collective-permute-start | bytes 56 | tf_op jit(solution)/shard_map/ppermute | solution.py:12
  138.5 10.0 %collective-permute-start.14 = (f32[4,128,128]{2,1,0:T(8,128)S(1)}, f32[4,128,128]{2,1,0:T(8,128)S(1)}, u32[]{:S(2)}, u32[]{:S(2)}) collective-permute-start(f32[4,128,128]{2,1,0:T(8,128)S(1)} %multiply_add_fusion.8), channel_id=1, source_target_pairs={{0,512},{8,520},{16,528},{24,536},{32,544},{40,552},{48,560},{56,5... | collective-permute-start | bytes 786440 | tf_op jit(solution)/shard_map/ppermute | solution.py:12
  143.3 5.2 %collective-permute-start.6 = (f32[4]{0:T(128)S(1)}, f32[4]{0:T(128)S(1)}, u32[]{:S(2)}, u32[]{:S(2)}) collective-permute-start(f32[4]{0:T(128)S(1)} %get-tuple-element.212), channel_id=1, source_target_pairs={{0,256},{8,264},{16,272},{24,280},{32,288},{40,296},{48,304},{56,3... | collective-permute-start | bytes 56 | tf_op jit(solution)/shard_map/ppermute | solution.py:12
  149.2 20.4 %copy-start = (bf16[128,512]{1,0:T(8,128)(2,1)S(1)}, bf16[128,512]{1,0:T(8,128)(2,1)}, u32[]{:S(2)}) copy-start(bf16[128,512]{1,0:T(8,128)(2,1)} %param.13) | copy-start | bytes 393220
  183.3 28.7 %collective-permute-start.22 = (f32[4,128,128]{2,1,0:T(8,128)S(1)}, f32[4,128,128]{2,1,0:T(8,128)S(1)}, u32[]{:S(2)}, u32[]{:S(2)}) collective-permute-start(f32[4,128,128]{2,1,0:T(8,128)S(1)} %fusion.72), channel_id=1, source_target_pairs={{8,0},{16,8},{24,16},{32,24},{40,32},{48,40},{56,48},{64,56},{72,6... | collective-permute-start | bytes 786440 | tf_op jit(solution)/shard_map/ppermute | solution.py:12
  212.0 13.7 %collective-permute-start.23 = (f32[4,128,128]{2,1,0:T(8,128)S(1)}, f32[4,128,128]{2,1,0:T(8,128)S(1)}, u32[]{:S(2)}, u32[]{:S(2)}) collective-permute-start(f32[4,128,128]{2,1,0:T(8,128)S(1)} %collective-permute-done.22), channel_id=1, source_target_pairs={{8,0},{16,8},{24,16},{32,24},{40,32},{48,40},{56,48},{64,56},{72,6... | collective-permute-start | bytes 786440 | tf_op jit(solution)/shard_map/ppermute | solution.py:12
  216.1 5.0 %collective-permute-start.15 = (f32[4]{0:T(128)S(1)}, f32[4]{0:T(128)S(1)}, u32[]{:S(2)}, u32[]{:S(2)}) collective-permute-start(f32[4]{0:T(128)S(1)} %slice_reduce_fusion), channel_id=1, source_target_pairs={{8,0},{16,8},{24,16},{32,24},{40,32},{48,40},{56,48},{64,56},{72,6... | collective-permute-start | bytes 56 | tf_op jit(solution)/shard_map/ppermute | solution.py:12
  221.1 4.6 %collective-permute-start.16 = (f32[4]{0:T(128)S(1)}, f32[4]{0:T(128)S(1)}, u32[]{:S(2)}, u32[]{:S(2)}) collective-permute-start(f32[4]{0:T(128)S(1)} %collective-permute-done.15), channel_id=1, source_target_pairs={{8,0},{16,8},{24,16},{32,24},{40,32},{48,40},{56,48},{64,56},{72,6... | collective-permute-start | bytes 56 | tf_op jit(solution)/shard_map/ppermute | solution.py:12
  225.8 17.3 %collective-permute-start.24 = (f32[4,128,128]{2,1,0:T(8,128)S(1)}, f32[4,128,128]{2,1,0:T(8,128)S(1)}, u32[]{:S(2)}, u32[]{:S(2)}) collective-permute-start(f32[4,128,128]{2,1,0:T(8,128)S(1)} %multiply_add_fusion.6), channel_id=1, source_target_pairs={{16,0},{24,8},{32,16},{40,24},{48,32},{56,40},{64,48},{72,56},{80,... | collective-permute-start | bytes 786440 | tf_op jit(solution)/shard_map/ppermute | solution.py:12
  243.1 26.4 %collective-permute-start.25 = (f32[4,128,128]{2,1,0:T(8,128)S(1)}, f32[4,128,128]{2,1,0:T(8,128)S(1)}, u32[]{:S(2)}, u32[]{:S(2)}) collective-permute-start(f32[4,128,128]{2,1,0:T(8,128)S(1)} %multiply_add_fusion.5), channel_id=1, source_target_pairs={{32,0},{40,8},{48,16},{56,24},{64,32},{72,40},{80,48},{88,56},{96,... | collective-permute-start | bytes 786440 | tf_op jit(solution)/shard_map/ppermute | solution.py:12
  251.2 18.3 %collective-permute-start.17 = (f32[4]{0:T(128)S(1)}, f32[4]{0:T(128)S(1)}, u32[]{:S(2)}, u32[]{:S(2)}) collective-permute-start(f32[4]{0:T(128)S(1)} %get-tuple-element.210), channel_id=1, source_target_pairs={{16,0},{24,8},{32,16},{40,24},{48,32},{56,40},{64,48},{72,56},{80,... | collective-permute-start | bytes 56 | tf_op jit(solution)/shard_map/ppermute | solution.py:12
  269.6 26.6 %collective-permute-start.26 = (f32[4,128,128]{2,1,0:T(8,128)S(1)}, f32[4,128,128]{2,1,0:T(8,128)S(1)}, u32[]{:S(2)}, u32[]{:S(2)}) collective-permute-start(f32[4,128,128]{2,1,0:T(8,128)S(1)} %multiply_add_fusion.4), channel_id=1, source_target_pairs={{64,0},{72,8},{80,16},{88,24},{96,32},{104,40},{112,48},{120,56},{... | collective-permute-start | bytes 786440 | tf_op jit(solution)/shard_map/ppermute | solution.py:12
  271.6 16.0 %collective-permute-start.18 = (f32[4]{0:T(128)S(1)}, f32[4]{0:T(128)S(1)}, u32[]{:S(2)}, u32[]{:S(2)}) collective-permute-start(f32[4]{0:T(128)S(1)} %get-tuple-element.208), channel_id=1, source_target_pairs={{32,0},{40,8},{48,16},{56,24},{64,32},{72,40},{80,48},{88,56},{96,... | collective-permute-start | bytes 56 | tf_op jit(solution)/shard_map/ppermute | solution.py:12
  296.3 24.6 %collective-permute-start.27 = (f32[4,128,128]{2,1,0:T(8,128)S(1)}, f32[4,128,128]{2,1,0:T(8,128)S(1)}, u32[]{:S(2)}, u32[]{:S(2)}) collective-permute-start(f32[4,128,128]{2,1,0:T(8,128)S(1)} %multiply_add_fusion.3), channel_id=1, source_target_pairs={{128,0},{136,8},{144,16},{152,24},{160,32},{168,40},{176,48},{184,... | collective-permute-start | bytes 786440 | tf_op jit(solution)/shard_map/ppermute | solution.py:12
  298.3 13.0 %collective-permute-start.19 = (f32[4]{0:T(128)S(1)}, f32[4]{0:T(128)S(1)}, u32[]{:S(2)}, u32[]{:S(2)}) collective-permute-start(f32[4]{0:T(128)S(1)} %get-tuple-element.206), channel_id=1, source_target_pairs={{64,0},{72,8},{80,16},{88,24},{96,32},{104,40},{112,48},{120,56},{... | collective-permute-start | bytes 56 | tf_op jit(solution)/shard_map/ppermute | solution.py:12
  311.3 19.3 %collective-permute-start.20 = (f32[4]{0:T(128)S(1)}, f32[4]{0:T(128)S(1)}, u32[]{:S(2)}, u32[]{:S(2)}) collective-permute-start(f32[4]{0:T(128)S(1)} %get-tuple-element.204), channel_id=1, source_target_pairs={{128,0},{136,8},{144,16},{152,24},{160,32},{168,40},{176,48},{184,... | collective-permute-start | bytes 56 | tf_op jit(solution)/shard_map/ppermute | solution.py:12
  321.0 24.3 %collective-permute-start.28 = (f32[4,128,128]{2,1,0:T(8,128)S(1)}, f32[4,128,128]{2,1,0:T(8,128)S(1)}, u32[]{:S(2)}, u32[]{:S(2)}) collective-permute-start(f32[4,128,128]{2,1,0:T(8,128)S(1)} %multiply_add_fusion.2), channel_id=1, source_target_pairs={{256,0},{264,8},{272,16},{280,24},{288,32},{296,40},{304,48},{312,... | collective-permute-start | bytes 786440 | tf_op jit(solution)/shard_map/ppermute | solution.py:12
  330.6 14.7 %collective-permute-start.21 = (f32[4]{0:T(128)S(1)}, f32[4]{0:T(128)S(1)}, u32[]{:S(2)}, u32[]{:S(2)}) collective-permute-start(f32[4]{0:T(128)S(1)} %get-tuple-element.202), channel_id=1, source_target_pairs={{256,0},{264,8},{272,16},{280,24},{288,32},{296,40},{304,48},{312,... | collective-permute-start | bytes 56 | tf_op jit(solution)/shard_map/ppermute | solution.py:12
  345.5 17.9 %collective-permute-start.29 = (f32[4,128,128]{2,1,0:T(8,128)S(1)}, f32[4,128,128]{2,1,0:T(8,128)S(1)}, u32[]{:S(2)}, u32[]{:S(2)}) collective-permute-start(f32[4,128,128]{2,1,0:T(8,128)S(1)} %multiply_add_fusion.1), channel_id=1, source_target_pairs={{512,0},{520,8},{528,16},{536,24},{544,32},{552,40},{560,48},{568,... | collective-permute-start | bytes 786440 | tf_op jit(solution)/shard_map/ppermute | solution.py:12
  (2 other events, 1.6 us)
where the time goes:
time: 367 us; the launch traced here: 366 us
  waiting for transfers between devices  177 us (48%)
  starting transfers between devices  139 us (38%)
  blocking collectives  32.7 us (9%)
  matrix products  7.26 us (2%)
  local copies, waits for them, and re-layouts  5.8 us (2%)
    ppermute x30, waiting for transfers between devices, passed_along(): return lax.ppermute(block, axis, route)  177 us
    ppermute x30, starting transfers between devices, passed_along(): return lax.ppermute(block, axis, route)  139 us
    psum x1, blocking collectives, local(): square_sum = lax.psum(jnp.sum(raw * raw, axis=1), 'head')  20.3 us
    psum x1, blocking collectives, local(): dot_sum = lax.psum(jnp.sum(upstream * normed, axis=1), 'head')  12.4 us
  transfers between devices with their start and end apart: 30, of which 23 were waited for; matrix products, arithmetic and copies ran while one was open for 2% of the time, Pallas kernels for 0%

commit v1 on v0

v1 whole, which is shorter than its diff:
```python
import functools

import jax
import jax.numpy as jnp
from jax import lax
from jax.experimental import pallas as pl
from jax.experimental.pallas import tpu as pltpu
from jax.sharding import PartitionSpec as P

ROW = 16
CHUNKS = 2
MESH = pl.DeviceIdType.MESH
F32 = jnp.float32
BF16 = jnp.bfloat16


def dot(a, b, dims, precision=None):
    return lax.dot_general(
        a, b, (dims, ((), ())), precision=precision, preferred_element_type=F32
    )


NN = ((1,), (0,))
NT = ((1,), (1,))
TN = ((0,), (0,))


def halves(x):
    high = x.astype(BF16)
    return high, (x - high.astype(F32)).astype(BF16)


def kernel(
    Y,
    Z,
    N,
    C,
    q_ref,
    k_ref,
    v_ref,
    ld_ref,
    ct_ref,
    att_ref,
    qg_ref,
    kg_ref,
    vg_ref,
    block,
    came,
    excl,
    state,
    tot_out,
    tot_in,
    fade_d,
    row_out,
    row_in,
    sums_out,
    sums_in,
    decay_s,
    weights_s,
    intra_s,
    raw_s,
    rg_s,
    sqt_s,
    growth_s,
    fade_s,
    in_ssem,
    in_rsem,
    out_ssem,
    out_rsem,
    y_ssem,
    y_rsem,
    t_ssem,
    t_rsem,
    x_ssem,
    x_rsem,
):
    H = ld_ref.shape[0]
    T = ld_ref.shape[1]
    D = q_ref.shape[1] // H
    rows = H * D // Z
    part = rows // C
    per_head = D // rows
    width = D * H * N
    seq = lax.axis_index("seq")
    mine = lax.axis_index("head")
    y = lax.div(seq, Z)
    z = lax.rem(seq, Z)

    barrier = pltpu.get_barrier_semaphore()

    def far_first(count, i):
        half = count // 2
        return half + jnp.where(lax.rem(i, 2) == 0, lax.div(i, 2), -lax.div(i + 1, 2))

    def peers(count, at, visit):
        def step(i, carry):
            visit(lax.rem(at + far_first(count, i), count))
            return carry

        lax.fori_loop(0, count - 1, step, 0)

    def z_device(other):
        return (y * Z + other, mine)

    def y_device(other):
        return (other * Z + z, mine)

    def x_device(other):
        return (seq, other)

    for count, at, device in ((Z, z, z_device), (Y, y, y_device), (N, mine, x_device)):

        def greet(other, device=device):
            pl.semaphore_signal(barrier, inc=1, device_id=device(other), device_id_type=MESH)

        peers(count, at, greet)

    t_i = lax.broadcasted_iota(jnp.int32, (T, T), 0)
    s_i = lax.broadcasted_iota(jnp.int32, (T, T), 1)
    causal = t_i >= s_i
    eye = t_i == s_i
    lower = causal.astype(F32)
    ld = ld_ref[...]
    cum_row = dot(ld, lower, NT, lax.Precision.HIGHEST)
    cum_col = dot(lower, ld, NT, lax.Precision.HIGHEST)
    totals = cum_row[:, T - 1 : T]

    def head(ref, h):
        return ref[:, h * D : (h + 1) * D]

    for h in range(H):
        total = totals[h : h + 1, :]
        tot_out[h] = jnp.broadcast_to(total, (1, D))
        column = cum_col[:, h : h + 1]
        fade = jnp.broadcast_to(jnp.exp(jnp.broadcast_to(total, (T, 1)) - column), (T, D))
        fade_s[h] = fade
        scaled = (head(k_ref, h).astype(F32) * fade).astype(BF16)
        block[0, h * D : (h + 1) * D, :] = dot(scaled, head(v_ref, h), TN)

    pl.semaphore_wait(barrier, (Z - 1) + (Y - 1) + (N - 1))

    def t_copy(other, src, slot):
        return pltpu.make_async_remote_copy(
            src_ref=tot_out.at[src],
            dst_ref=tot_in.at[slot],
            send_sem=t_ssem.at[other],
            recv_sem=t_rsem.at[slot],
            device_id=z_device(other),
            device_id_type=MESH,
        )

    peers(Z, z, lambda other: t_copy(other, lax.div(other, per_head), z).start())
    tot_in[z] = tot_out[lax.div(z, per_head)]

    def in_copy(w, c, other, slot):
        return pltpu.make_async_remote_copy(
            src_ref=block.at[w, pl.ds(pl.multiple_of(other * rows + c * part, part), part)],
            dst_ref=came.at[w, slot, pl.ds(c * part, part)],
            send_sem=in_ssem.at[w, c, other],
            recv_sem=in_rsem.at[w, c, slot],
            device_id=z_device(other),
            device_id_type=MESH,
        )

    def out_copy(w, c, other, slot):
        return pltpu.make_async_remote_copy(
            src_ref=excl.at[w, other, pl.ds(c * part, part)],
            dst_ref=state.at[w, pl.ds(pl.multiple_of(slot * rows + c * part, part), part)],
            send_sem=out_ssem.at[w, c, other],
            recv_sem=out_rsem.at[w, c, slot],
            device_id=z_device(other),
            device_id_type=MESH,
        )

    def y_copy(w, c, other, slot):
        return pltpu.make_async_remote_copy(
            src_ref=row_out.at[w, c],
            dst_ref=row_in.at[w, c, slot],
            send_sem=y_ssem.at[w, c, other],
            recv_sem=y_rsem.at[w, c, slot],
            device_id=y_device(other),
            device_id_type=MESH,
        )

    def x_copy(other, slot):
        return pltpu.make_async_remote_copy(
            src_ref=sums_out,
            dst_ref=sums_in.at[slot],
            send_sem=x_ssem.at[other],
            recv_sem=x_rsem.at[slot],
            device_id=x_device(other),
            device_id_type=MESH,
        )

    def enter(w):
        for c in range(C):
            peers(Z, z, lambda other: in_copy(w, c, other, z).start())
        came[w, z] = block[w, pl.ds(pl.multiple_of(z * rows, rows), rows), :]

    def scan(w):
        for c in range(C):
            peers(Z, z, lambda other: in_copy(w, c, other, other).wait_recv())
            if w == 0 and c == 0:
                peers(Z, z, lambda other: t_copy(other, 0, other).wait_recv())
            piece = slice(c * part, (c + 1) * part)

            def step(i, carry):
                total, passed = carry
                at = i if w == 0 else Z - 1 - i
                excl[w, at, piece, :] = total
                if c == 0:
                    fade_d[w, at] = passed
                one = tot_in[at]
                total = jnp.exp(one) * total + came[w, at, piece, :]
                return total, passed + one

            total, passed = lax.fori_loop(
                0, Z, step, (jnp.zeros((part, D), F32), jnp.zeros((1, D), F32)), unroll=4
            )
            row_out[w, c, 0:part, :] = total
            row_out[w, c, part : part + 8, :] = jnp.broadcast_to(passed, (8, D))
            peers(Y, y, lambda other: y_copy(w, c, other, y).start())
        for c in range(C):
            piece = slice(c * part, (c + 1) * part)
            peers(Y, y, lambda other: y_copy(w, c, other, other).wait_recv())
            row_in[w, c, y] = row_out[w, c]
            before = jnp.zeros((part, D), F32)
            for i in range(Y):
                at = i if w == 0 else Y - 1 - i
                grown = jnp.exp(row_in[w, c, at, part : part + 1, :]) * before
                grown = grown + row_in[w, c, at, 0:part, :]
                use = y > at if w == 0 else y < at
                before = jnp.where(use, grown, before)

            def finish(other):
                excl[w, other, piece, :] = (
                    excl[w, other, piece, :] + jnp.exp(fade_d[w, other]) * before
                )

            def leave(other):
                finish(other)
                out_copy(w, c, other, z).start()

            peers(Z, z, leave)
            finish(z)
        state[w, pl.ds(pl.multiple_of(z * rows, rows), rows), :] = excl[w, z]
        for c in range(C):
            peers(Z, z, lambda other: out_copy(w, c, other, other).wait_recv())

    enter(0)

    for h in range(H):
        column = jnp.broadcast_to(cum_col[:, h : h + 1], (T, T))
        growth = jnp.exp(column)
        growth_s[h] = growth
        spread = column - cum_row[h : h + 1, :]
        decay = jnp.where(causal, jnp.exp(jnp.minimum(spread, 0.0)), 0.0)
        decay_s[h] = decay
        weights = (dot(head(q_ref, h), head(k_ref, h), NT) * decay).astype(BF16)
        weights_s[h] = weights
        intra_s[h] = dot(weights, head(v_ref, h), NN)
        scaled = head(q_ref, h).astype(F32) * growth
        high, low = halves(scaled.T)
        sqt_s[h, :, 0:T] = high
        sqt_s[h, :, T : 2 * T] = low

    scan(0)

    squares = jnp.zeros((T, D), F32)
    inner = jnp.zeros((T, D), F32)
    for h in range(H):
        high, low = halves(state[0, h * D : (h + 1) * D, :])
        q_one = head(q_ref, h)
        carried = dot(
            jnp.concatenate([q_one, q_one], axis=1), jnp.concatenate([high, low], axis=0), NN
        )
        raw = growth_s[h] * carried + intra_s[h]
        raw_s[h] = raw
        squares = squares + raw * raw
        inner = inner + raw * head(ct_ref, h).astype(F32)

    def to_row(x):
        column = jnp.sum(x, axis=1, keepdims=True)
        return jnp.sum(jnp.where(eye, column, 0.0), axis=0, keepdims=True)

    def to_column(x):
        return jnp.sum(jnp.where(eye, x, 0.0), axis=1, keepdims=True)

    sums_out[0:1, :] = to_row(squares)
    sums_out[1:2, :] = to_row(inner)
    peers(N, mine, lambda other: x_copy(other, mine).start())
    sums_in[mine] = sums_out[...]
    peers(N, mine, lambda other: x_copy(other, other).wait_recv())
    gathered = sums_in[0]
    for i in range(1, N):
        gathered = gathered + sums_in[i]
    inverse_row = lax.rsqrt(gathered[0:1, :] / width + 1e-06)
    dot_row = inverse_row * gathered[1:2, :] / width
    inverse = jnp.broadcast_to(to_column(inverse_row), (T, D))
    mean_dot = jnp.broadcast_to(to_column(dot_row), (T, D))
    for h in range(H):
        normed = raw_s[h] * inverse
        raw_s[h] = normed
        grad = (inverse * (head(ct_ref, h).astype(F32) - normed * mean_dot)).astype(BF16)
        rg_s[h] = grad
        block[1, h * D : (h + 1) * D, :] = dot(
            sqt_s[h], jnp.concatenate([grad, grad], axis=0), NN
        )

    enter(1)

    for h in range(H):
        columns = slice(h * D, (h + 1) * D)
        att_ref[:, columns] = raw_s[h].astype(BF16)
        grad = rg_s[h]
        high, low = halves(state[0, h * D : (h + 1) * D, :])
        grad_weights = (dot(grad, head(v_ref, h), NT) * decay_s[h]).astype(BF16)
        carried = dot(
            jnp.concatenate([grad, grad], axis=1), jnp.concatenate([high, low], axis=1), NT
        )
        query_total = growth_s[h] * carried + dot(grad_weights, head(k_ref, h), NN)
        qg_ref[:, columns] = query_total.astype(BF16)
        raw_s[h] = dot(grad_weights, head(q_ref, h), TN)
        intra_s[h] = dot(weights_s[h], grad, TN)

    scan(1)

    for h in range(H):
        columns = slice(h * D, (h + 1) * D)
        high, low = halves(state[1, h * D : (h + 1) * D, :])
        v_one = head(v_ref, h)
        k_one = head(k_ref, h)
        key_part = dot(
            jnp.concatenate([v_one, v_one], axis=1), jnp.concatenate([high, low], axis=1), NT
        )
        value_part = dot(
            jnp.concatenate([k_one, k_one], axis=1), jnp.concatenate([high, low], axis=0), NN
        )
        kg_ref[:, columns] = (raw_s[h] + fade_s[h] * key_part).astype(BF16)
        vg_ref[:, columns] = (intra_s[h] + fade_s[h] * value_part).astype(BF16)

    peers(Z, z, lambda other: t_copy(other, 0, other).wait_send())
    for w in range(2):
        for c in range(C):
            peers(Z, z, lambda other: in_copy(w, c, other, other).wait_send())
            peers(Y, y, lambda other: y_copy(w, c, other, other).wait_send())
            peers(Z, z, lambda other: out_copy(w, c, other, other).wait_send())
    peers(N, mine, lambda other: x_copy(other, other).wait_send())


def local(query_rows, key_rows, value_rows, log_decay, cotangent):
    H, T = log_decay.shape
    D = query_rows.shape[1] // H
    length = lax.axis_size("seq")
    N = lax.axis_size("head")
    Z = ROW
    Y = length // Z
    C = CHUNKS
    rows = H * D // Z
    part = rows // C
    vmem = pl.BlockSpec(memory_space=pltpu.VMEM)
    dma = pltpu.SemaphoreType.DMA
    out = jax.ShapeDtypeStruct(query_rows.shape, BF16)
    return pl.pallas_call(
        functools.partial(kernel, Y, Z, N, C),
        out_shape=(out,) * 4,
        in_specs=[vmem] * 5,
        out_specs=(vmem,) * 4,
        scratch_shapes=[
            pltpu.VMEM((2, H * D, D), F32),
            pltpu.VMEM((2, Z, rows, D), F32),
            pltpu.VMEM((2, Z, rows, D), F32),
            pltpu.VMEM((2, H * D, D), F32),
            pltpu.VMEM((H, 1, D), F32),
            pltpu.VMEM((Z, 1, D), F32),
            pltpu.VMEM((2, Z, 1, D), F32),
            pltpu.VMEM((2, C, part + 8, D), F32),
            pltpu.VMEM((2, C, Y, part + 8, D), F32),
            pltpu.VMEM((8, T), F32),
            pltpu.VMEM((N, 8, T), F32),
            pltpu.VMEM((H, T, T), F32),
            pltpu.VMEM((H, T, T), BF16),
            pltpu.VMEM((H, T, D), F32),
            pltpu.VMEM((H, T, D), F32),
            pltpu.VMEM((H, T, D), BF16),
            pltpu.VMEM((H, D, 2 * T), BF16),
            pltpu.VMEM((H, T, D), F32),
            pltpu.VMEM((H, T, D), F32),
            dma((2, C, Z)),
            dma((2, C, Z)),
            dma((2, C, Z)),
            dma((2, C, Z)),
            dma((2, C, Y)),
            dma((2, C, Y)),
            dma((Z,)),
            dma((Z,)),
            dma((N,)),
            dma((N,)),
        ],
        compiler_params=pltpu.CompilerParams(collective_id=0, has_side_effects=True),
    )(query_rows, key_rows, value_rows, log_decay, cotangent)


def solution(mesh):
    return jax.shard_map(
        local,
        mesh=mesh,
        in_specs=(
            P("seq", "head"),
            P("seq", "head"),
            P("seq", "head"),
            P("head", "seq"),
            P("seq", "head"),
        ),
        out_specs=(P("seq", "head"), P("seq", "head"), P("seq", "head"), P("seq", "head")),
        check_vma=False,
    )
```

time: 367 us -> 98.9 us (0.27)
  the two profiles are of different devices: /device:TPU:81 before, /device:TPU:8 now
where the time goes in v1:
time: 98.9 us; the launch traced here: 98.6 us
  Pallas kernels  93.8 us (95%)
  local copies, waits for them, and re-layouts  4.16 us (4%)
    pallas_call x1, Pallas kernels, local(): pl.pallas_call(functools.partial(kernel, Y, Z, N, C), out_shape=(out,) *...  93.8 us
    unnamed x10, local copies, waits for them, and re-layouts  4.16 us

profile of v1, /device:TPU:8, one launch (start us, length us, event | category | flops | bytes accessed | tf_op | source)
XLA Modules:
  0.0 98.6 jit_solution(17100934961863947704)
XLA Ops:
  0.6 93.8 %shard_map.84 = (bf16[128,512]{1,0:T(8,128)(2,1)}, bf16[128,512]{1,0:T(8,128)(2,1)}, bf16[128,512]{1,0:T(8,128)(2,1)}, bf16[128,512]{1,0:T(8,128)(2,1)}) custom-call(bf16[128,512]{1,0:T(8,128)(2,1)} %q_ref.1, bf16[128,512]{1,0:T(8,128)(2,1)} %k_ref.1, bf16[128,512]{1,0:T(8,128)(2,1)} %v_ref.1, f32[4,128]{1,0:T(4,128)} %ld_ref.1, bf16[128,512]{1,0:T(8,128)(2,1)} %ct_ref.1), custom_call_target="tpu_custom_call" | custom-call | tf_op jit(solution)/shard_map/pallas_call | solution.py:364
  94.5 0.0 copy-start.2
  94.5 1.6 %copy.13 = bf16[128,512]{1,0:T(8,128)(2,1)} copy(bf16[128,512]{1,0:T(8,128)(2,1)} %get-tuple-element.8) | data formatting | bytes 262144
  96.1 0.0 copy-done.2
  96.1 0.0 copy-start.1
  96.1 0.7 copy.14
  96.7 0.3 copy-done.1
  97.0 0.0 copy-start
  97.0 0.7 copy.15
  97.7 0.3 copy-done
  98.0 0.7 copy.16
Async XLA Ops:
  94.5 1.6 %copy-start.2 = (bf16[128,512]{1,0:T(8,128)(2,1)S(1)}, bf16[128,512]{1,0:T(8,128)(2,1)}, u32[]{:S(2)}) copy-start(bf16[128,512]{1,0:T(8,128)(2,1)} %get-tuple-element.9) | copy-start | bytes 393220
  96.1 1.0 copy-start.1
  97.0 1.0 copy-start

commit v2 on v1

v2 whole, which is shorter than its diff:
```python
import functools

import jax
import jax.numpy as jnp
from jax import lax
from jax.experimental import pallas as pl
from jax.experimental.pallas import tpu as pltpu
from jax.sharding import PartitionSpec as P

ROW = 16
CHUNKS = 2
MESH = pl.DeviceIdType.MESH
F32 = jnp.float32
BF16 = jnp.bfloat16


def dot(a, b, dims, precision=None):
    return lax.dot_general(
        a, b, (dims, ((), ())), precision=precision, preferred_element_type=F32
    )


NN = ((1,), (0,))
NT = ((1,), (1,))
TN = ((0,), (0,))


def halves(x):
    high = x.astype(BF16)
    return high, (x - high.astype(F32)).astype(BF16)


def kernel(
    Y,
    Z,
    N,
    C,
    q_ref,
    k_ref,
    v_ref,
    ld_ref,
    ct_ref,
    att_ref,
    qg_ref,
    kg_ref,
    vg_ref,
    block,
    other_s,
    both_s,
    came,
    excl,
    pref,
    ahead,
    state,
    tot_s,
    tot_in,
    two_s,
    two_in,
    fade_d,
    row_out,
    row_in,
    sums_out,
    sums_in,
    decay_s,
    weights_s,
    intra_s,
    raw_s,
    rg_s,
    sqt_s,
    growth_s,
    fade_s,
    p_ssem,
    p_rsem,
    in_ssem,
    in_rsem,
    out_ssem,
    out_rsem,
    f_ssem,
    f_rsem,
    y_ssem,
    y_rsem,
    t_ssem,
    t_rsem,
    two_ssem,
    two_rsem,
    x_ssem,
    x_rsem,
):
    H = ld_ref.shape[0]
    T = ld_ref.shape[1]
    D = q_ref.shape[1] // H
    M = Z // 2
    size = H * D // (2 * C)
    part = size // M
    width = D * H * N
    seq = lax.axis_index("seq")
    mine = lax.axis_index("head")
    y = lax.div(seq, Z)
    z = lax.rem(seq, Z)
    m = lax.div(z, 2)
    b = lax.rem(z, 2)
    partner = z + 1 - 2 * b

    barrier = pltpu.get_barrier_semaphore()

    def far_first(count, i):
        half = count // 2
        return half + jnp.where(lax.rem(i, 2) == 0, lax.div(i, 2), -lax.div(i + 1, 2))

    def peers(count, at, visit):
        def step(i, carry):
            visit(lax.rem(at + far_first(count, i), count))
            return carry

        lax.fori_loop(0, count - 1, step, 0)

    def across(visit, near_first=False):
        def step(i, carry):
            i = M - 1 - i if near_first else i
            reach = 2 * (M // 2 - lax.div(i, 2)) - 1
            offset = jnp.where(lax.rem(i, 2) == 0, reach, Z - reach)
            visit(lax.rem(z + offset, Z))
            return carry

        lax.fori_loop(0, M, step, 0)

    def z_device(other):
        return (y * Z + other, mine)

    def y_device(other):
        return (other * Z + z, mine)

    def x_device(other):
        return (seq, other)

    def greet(device):
        pl.semaphore_signal(barrier, inc=1, device_id=device, device_id_type=MESH)

    across(lambda other: greet(z_device(other)))
    peers(Y, y, lambda other: greet(y_device(other)))
    peers(N, mine, lambda other: greet(x_device(other)))

    t_i = lax.broadcasted_iota(jnp.int32, (T, T), 0)
    s_i = lax.broadcasted_iota(jnp.int32, (T, T), 1)
    causal = t_i >= s_i
    eye = t_i == s_i
    lower = causal.astype(F32)
    ld = ld_ref[...]
    cum_row = dot(ld, lower, NT, lax.Precision.HIGHEST)
    cum_col = dot(lower, ld, NT, lax.Precision.HIGHEST)
    totals = cum_row[:, T - 1 : T]

    def head(ref, h):
        return ref[:, h * D : (h + 1) * D]

    def remote(src, dst, send, recv, device):
        return pltpu.make_async_remote_copy(
            src_ref=src,
            dst_ref=dst,
            send_sem=send,
            recv_sem=recv,
            device_id=device,
            device_id_type=MESH,
        )

    def span(half, c):
        return pl.ds(pl.multiple_of((half * C + c) * size, size), size)

    def strip(slot):
        return pl.ds(pl.multiple_of(slot * part, part), part)

    def t_copy():
        return remote(tot_s, tot_in, t_ssem, t_rsem, z_device(partner))

    def pair_copy(w, c):
        return remote(
            block.at[w, span(1 - b, c)],
            other_s.at[w, c],
            p_ssem.at[w, c],
            p_rsem.at[w, c],
            z_device(partner),
        )

    def two_copy(other, slot):
        at = lax.div(other, 2)
        return remote(
            two_s, two_in.at[slot], two_ssem.at[at], two_rsem.at[slot], z_device(other)
        )

    def in_copy(w, c, other, slot):
        at = lax.div(other, 2)
        return remote(
            both_s.at[w, c, strip(at)],
            came.at[w, c, slot],
            in_ssem.at[w, c, at],
            in_rsem.at[w, c, slot],
            z_device(other),
        )

    def out_copy(w, c, other, slot):
        at = lax.div(other, 2)
        return remote(
            excl.at[w, c, at],
            pref.at[w, c, strip(slot)],
            out_ssem.at[w, c, at],
            out_rsem.at[w, c, slot],
            z_device(other),
        )

    def forward_copy(w, c, half, slot):
        row = pl.multiple_of((half * C + c) * size + slot * part, part)
        return remote(
            ahead.at[w, c, strip(slot)],
            state.at[w, pl.ds(row, part)],
            f_ssem.at[w, c, slot],
            f_rsem.at[w, c, slot],
            z_device(partner),
        )

    def y_copy(w, c, other, slot):
        return remote(
            row_out.at[w, c],
            row_in.at[w, c, slot],
            y_ssem.at[w, c, other],
            y_rsem.at[w, c, slot],
            y_device(other),
        )

    def x_copy(other, slot):
        return remote(
            sums_out, sums_in.at[slot], x_ssem.at[other], x_rsem.at[slot], x_device(other)
        )

    def half_of(other):
        return lax.div(other, 2)

    def enter(w):
        for c in range(C):
            pair_copy(w, c).wait_recv()
            own = block[w, span(b, c), :]
            given = other_s[w, c]
            own_leads = b == w
            lead = jnp.where(own_leads, own, given)
            trail = jnp.where(own_leads, given, own)
            mine_t = tot_s[b * C + c]
            given_t = tot_in[b * C + c]
            trail_t = jnp.where(own_leads, given_t, mine_t)
            both_s[w, c] = jnp.exp(trail_t) * lead + trail
            across(lambda other: in_copy(w, c, other, m).start())

    def scan(w):
        for c in range(C):
            if w == 0 and c == 0:
                across(lambda other: two_copy(other, half_of(other)).wait_recv())
            across(lambda other: in_copy(w, c, other, half_of(other)).wait_recv())

            def step(i, carry):
                total, passed = carry
                at = i if w == 0 else M - 1 - i
                excl[w, c, at] = total
                fade_d[w, c, at] = passed
                one = two_in[at, c]
                total = jnp.exp(one) * total + came[w, c, at]
                return total, passed + one

            total, passed = lax.fori_loop(
                0, M, step, (jnp.zeros((part, D), F32), jnp.zeros((1, D), F32)), unroll=True
            )
            row_out[w, c, 0:part, :] = total
            row_out[w, c, part : part + 8, :] = jnp.broadcast_to(passed, (8, D))
            peers(Y, y, lambda other: y_copy(w, c, other, y).start())
        for c in range(C):
            peers(Y, y, lambda other: y_copy(w, c, other, other).wait_recv())
            row_in[w, c, y] = row_out[w, c]
            before = jnp.zeros((part, D), F32)
            for i in range(Y):
                at = i if w == 0 else Y - 1 - i
                grown = jnp.exp(row_in[w, c, at, part : part + 1, :]) * before
                grown = grown + row_in[w, c, at, 0:part, :]
                use = y > at if w == 0 else y < at
                before = jnp.where(use, grown, before)

            def leave(other):
                at = half_of(other)
                excl[w, c, at] = excl[w, c, at] + jnp.exp(fade_d[w, c, at]) * before
                out_copy(w, c, other, m).start()

            across(leave)
        for c in range(C):
            own_leads = b == w
            mine_t = tot_s[b * C + c]
            given_t = tot_in[b * C + c]
            lead_t = jnp.exp(jnp.where(own_leads, mine_t, given_t))

            def land(other):
                slot = half_of(other)
                out_copy(w, c, other, slot).wait_recv()
                row = pl.multiple_of((b * C + c) * size + slot * part, part)
                own = block[w, pl.ds(row, part), :]
                given = other_s[w, c, strip(slot), :]
                lead = jnp.where(own_leads, own, given)
                first = pref[w, c, strip(slot), :]
                second = lead_t * first + lead
                ahead[w, c, strip(slot), :] = jnp.where(own_leads, second, first)
                forward_copy(w, c, b, slot).start()
                state[w, pl.ds(row, part), :] = jnp.where(own_leads, first, second)

            across(land, near_first=True)
        for c in range(C):
            across(lambda other: forward_copy(w, c, 1 - b, half_of(other)).wait_recv())

    totals = [jnp.broadcast_to(totals[h : h + 1, :], (1, D)) for h in range(H)]
    for h in range(H):
        tot_s[h] = totals[h]
    order = [half * C + c for c in range(C) for half in range(2)]
    for h in order:
        column = cum_col[:, h : h + 1]
        fade = jnp.exp(totals[h] - jnp.broadcast_to(column, (T, D)))
        fade_s[h] = fade
        scaled = (head(k_ref, h).astype(F32) * fade).astype(BF16)
        block[0, h * D : (h + 1) * D, :] = dot(scaled, head(v_ref, h), TN)

    pl.semaphore_wait(barrier, M + (Y - 1) + (N - 1))

    t_copy().start()
    for c in range(C):
        pair_copy(0, c).start()
    t_copy().wait_recv()
    for c in range(C):
        two_s[c] = tot_s[b * C + c] + tot_in[b * C + c]
    across(lambda other: two_copy(other, m).start())
    enter(0)

    for h in range(H):
        column = jnp.broadcast_to(cum_col[:, h : h + 1], (T, T))
        growth = jnp.exp(column)
        growth_s[h] = growth
        spread = column - cum_row[h : h + 1, :]
        decay = jnp.where(causal, jnp.exp(jnp.minimum(spread, 0.0)), 0.0)
        decay_s[h] = decay
        weights = (dot(head(q_ref, h), head(k_ref, h), NT) * decay).astype(BF16)
        weights_s[h] = weights
        intra_s[h] = dot(weights, head(v_ref, h), NN)
        scaled = head(q_ref, h).astype(F32) * growth
        high, low = halves(scaled.T)
        sqt_s[h, :, 0:T] = high
        sqt_s[h, :, T : 2 * T] = low

    scan(0)

    squares = jnp.zeros((T, D), F32)
    inner = jnp.zeros((T, D), F32)
    for h in range(H):
        high, low = halves(state[0, h * D : (h + 1) * D, :])
        q_one = head(q_ref, h)
        carried = dot(
            jnp.concatenate([q_one, q_one], axis=1), jnp.concatenate([high, low], axis=0), NN
        )
        raw = growth_s[h] * carried + intra_s[h]
        raw_s[h] = raw
        squares = squares + raw * raw
        inner = inner + raw * head(ct_ref, h).astype(F32)

    def to_row(x):
        column = jnp.sum(x, axis=1, keepdims=True)
        return jnp.sum(jnp.where(eye, column, 0.0), axis=0, keepdims=True)

    def to_column(x):
        return jnp.sum(jnp.where(eye, x, 0.0), axis=1, keepdims=True)

    sums_out[0:1, :] = to_row(squares)
    sums_out[1:2, :] = to_row(inner)
    peers(N, mine, lambda other: x_copy(other, mine).start())
    sums_in[mine] = sums_out[...]
    peers(N, mine, lambda other: x_copy(other, other).wait_recv())
    gathered = sums_in[0]
    for i in range(1, N):
        gathered = gathered + sums_in[i]
    inverse_row = lax.rsqrt(gathered[0:1, :] / width + 1e-06)
    dot_row = inverse_row * gathered[1:2, :] / width
    inverse = jnp.broadcast_to(to_column(inverse_row), (T, D))
    mean_dot = jnp.broadcast_to(to_column(dot_row), (T, D))
    for c in range(C):
        for h in (c, C + c):
            normed = raw_s[h] * inverse
            raw_s[h] = normed
            grad = (inverse * (head(ct_ref, h).astype(F32) - normed * mean_dot)).astype(BF16)
            rg_s[h] = grad
            block[1, h * D : (h + 1) * D, :] = dot(
                sqt_s[h], jnp.concatenate([grad, grad], axis=0), NN
            )
        pair_copy(1, c).start()

    enter(1)

    for h in range(H):
        columns = slice(h * D, (h + 1) * D)
        att_ref[:, columns] = raw_s[h].astype(BF16)
        grad = rg_s[h]
        high, low = halves(state[0, h * D : (h + 1) * D, :])
        grad_weights = (dot(grad, head(v_ref, h), NT) * decay_s[h]).astype(BF16)
        carried = dot(
            jnp.concatenate([grad, grad], axis=1), jnp.concatenate([high, low], axis=1), NT
        )
        query_total = growth_s[h] * carried + dot(grad_weights, head(k_ref, h), NN)
        qg_ref[:, columns] = query_total.astype(BF16)
        raw_s[h] = dot(grad_weights, head(q_ref, h), TN)
        intra_s[h] = dot(weights_s[h], grad, TN)

    scan(1)

    for h in range(H):
        columns = slice(h * D, (h + 1) * D)
        high, low = halves(state[1, h * D : (h + 1) * D, :])
        v_one = head(v_ref, h)
        k_one = head(k_ref, h)
        key_part = dot(
            jnp.concatenate([v_one, v_one], axis=1), jnp.concatenate([high, low], axis=1), NT
        )
        value_part = dot(
            jnp.concatenate([k_one, k_one], axis=1), jnp.concatenate([high, low], axis=0), NN
        )
        kg_ref[:, columns] = (raw_s[h] + fade_s[h] * key_part).astype(BF16)
        vg_ref[:, columns] = (intra_s[h] + fade_s[h] * value_part).astype(BF16)

    t_copy().wait_send()
    across(lambda other: two_copy(other, m).wait_send())
    for w in range(2):
        for c in range(C):
            pair_copy(w, c).wait_send()
            across(lambda other: in_copy(w, c, other, m).wait_send())
            peers(Y, y, lambda other: y_copy(w, c, other, y).wait_send())
            across(lambda other: out_copy(w, c, other, m).wait_send())
            across(lambda other: forward_copy(w, c, b, half_of(other)).wait_send())
    peers(N, mine, lambda other: x_copy(other, mine).wait_send())


def hand_over(a_ref, b_ref, c_ref, d_ref, a_out, b_out, c_out, d_out):
    a_out[...] = a_ref[...]
    b_out[...] = b_ref[...]
    c_out[...] = c_ref[...]
    d_out[...] = d_ref[...]


def local(query_rows, key_rows, value_rows, log_decay, cotangent):
    H, T = log_decay.shape
    D = query_rows.shape[1] // H
    length = lax.axis_size("seq")
    N = lax.axis_size("head")
    Z = ROW
    Y = length // Z
    C = CHUNKS
    M = Z // 2
    size = H * D // (2 * C)
    part = size // M
    vmem = pl.BlockSpec(memory_space=pltpu.VMEM)
    dma = pltpu.SemaphoreType.DMA
    out = jax.ShapeDtypeStruct(query_rows.shape, BF16)
    results = pl.pallas_call(
        functools.partial(kernel, Y, Z, N, C),
        out_shape=(out,) * 4,
        in_specs=[vmem] * 5,
        out_specs=(vmem,) * 4,
        scratch_shapes=[
            pltpu.VMEM((2, H * D, D), F32),
            pltpu.VMEM((2, C, size, D), F32),
            pltpu.VMEM((2, C, size, D), F32),
            pltpu.VMEM((2, C, M, part, D), F32),
            pltpu.VMEM((2, C, M, part, D), F32),
            pltpu.VMEM((2, C, size, D), F32),
            pltpu.VMEM((2, C, size, D), F32),
            pltpu.VMEM((2, H * D, D), F32),
            pltpu.VMEM((H, 1, D), F32),
            pltpu.VMEM((H, 1, D), F32),
            pltpu.VMEM((C, 1, D), F32),
            pltpu.VMEM((M, C, 1, D), F32),
            pltpu.VMEM((2, C, M, 1, D), F32),
            pltpu.VMEM((2, C, part + 8, D), F32),
            pltpu.VMEM((2, C, Y, part + 8, D), F32),
            pltpu.VMEM((8, T), F32),
            pltpu.VMEM((N, 8, T), F32),
            pltpu.VMEM((H, T, T), F32),
            pltpu.VMEM((H, T, T), BF16),
            pltpu.VMEM((H, T, D), F32),
            pltpu.VMEM((H, T, D), F32),
            pltpu.VMEM((H, T, D), BF16),
            pltpu.VMEM((H, D, 2 * T), BF16),
            pltpu.VMEM((H, T, D), F32),
            pltpu.VMEM((H, T, D), F32),
            dma((2, C)),
            dma((2, C)),
            dma((2, C, M)),
            dma((2, C, M)),
            dma((2, C, M)),
            dma((2, C, M)),
            dma((2, C, M)),
            dma((2, C, M)),
            dma((2, C, Y)),
            dma((2, C, Y)),
            dma,
            dma,
            dma((M,)),
            dma((M,)),
            dma((N,)),
            dma((N,)),
        ],
        compiler_params=pltpu.CompilerParams(collective_id=0, has_side_effects=True),
    )(query_rows, key_rows, value_rows, log_decay, cotangent)
    return pl.pallas_call(
        hand_over,
        out_shape=(out,) * 4,
        in_specs=[vmem] * 4,
        out_specs=(vmem,) * 4,
    )(*results)


def solution(mesh):
    return jax.shard_map(
        local,
        mesh=mesh,
        in_specs=(
            P("seq", "head"),
            P("seq", "head"),
            P("seq", "head"),
            P("head", "seq"),
            P("seq", "head"),
        ),
        out_specs=(P("seq", "head"), P("seq", "head"), P("seq", "head"), P("seq", "head")),
        check_vma=False,
    )
```

time: 98.9 us -> 93.6 us (0.946)
  the two profiles are of different devices: /device:TPU:8 before, /device:TPU:2 now
where the time goes in v2:
time: 93.6 us; the launch traced here: 93.5 us
  Pallas kernels  92.8 us (99%)
    pallas_call x1, Pallas kernels, local(): pl.pallas_call(functools.partial(kernel, Y, Z, N, C), out_shape=(out,) *...  90.9 us
    pallas_call x1, Pallas kernels, local(): pl.pallas_call(hand_over, out_shape=(out,) * 4, in_specs=[vmem] * 4, out_...  1.89 us

profile of v2, /device:TPU:2, one launch (start us, length us, event | category | flops | bytes accessed | tf_op | source)
XLA Modules:
  0.0 93.5 jit_solution(6530945577591333257)
XLA Ops:
  0.6 90.9 %shard_map.84 = (bf16[128,512]{1,0:T(8,128)(2,1)}, bf16[128,512]{1,0:T(8,128)(2,1)}, bf16[128,512]{1,0:T(8,128)(2,1)}, bf16[128,512]{1,0:T(8,128)(2,1)}) custom-call(bf16[128,512]{1,0:T(8,128)(2,1)} %q_ref.1, bf16[128,512]{1,0:T(8,128)(2,1)} %k_ref.1, bf16[128,512]{1,0:T(8,128)(2,1)} %v_ref.1, f32[4,128]{1,0:T(4,128)} %ld_ref.1, bf16[128,512]{1,0:T(8,128)(2,1)} %ct_ref.1), custom_call_target="tpu_custom_call" | custom-call | tf_op jit(solution)/shard_map/pallas_call | solution.py:459
  91.6 1.9 %shard_map.85 = (bf16[128,512]{1,0:T(8,128)(2,1)}, bf16[128,512]{1,0:T(8,128)(2,1)}, bf16[128,512]{1,0:T(8,128)(2,1)}, bf16[128,512]{1,0:T(8,128)(2,1)}) custom-call(bf16[128,512]{1,0:T(8,128)(2,1)} %get-tuple-element.8.a_ref, bf16[128,512]{1,0:T(8,128)(2,1)} %get-tuple-element.9.b_ref, bf16[128,512]{1,0:T(8,128)(2,1)} %get-tuple-element.10.c_ref, ...), custom_call_target="tpu_custom_call" | custom-call | tf_op jit(solution)/shard_map/pallas_call | solution.py:509

commit v3 on v2

--- a/solution.py
+++ b/solution.py
@@ -35,6 +35,15 @@
     Z,
     N,
     C,
+    q_hbm,
+    k_hbm,
+    v_hbm,
+    ld_hbm,
+    ct_hbm,
+    att_hbm,
+    qg_hbm,
+    kg_hbm,
+    vg_hbm,
     q_ref,
     k_ref,
     v_ref,
@@ -44,6 +53,9 @@
     qg_ref,
     kg_ref,
     vg_ref,
+    load_sem,
+    save_sem,
+    grad_sem,
     block,
     other_s,
     both_s,
@@ -101,6 +113,18 @@
     b = lax.rem(z, 2)
     partner = z + 1 - 2 * b
 
+    loads = [
+        pltpu.make_async_copy(src, dst, load_sem.at[i])
+        for i, (src, dst) in enumerate(
+            (
+                (ld_hbm, ld_ref),
+                (k_hbm, k_ref),
+                (v_hbm, v_ref),
+                (q_hbm, q_ref),
+                (ct_hbm, ct_ref),
+            )
+        )
+    ]
     barrier = pltpu.get_barrier_semaphore()
 
     def far_first(count, i):
@@ -124,6 +148,13 @@
 
         lax.fori_loop(0, M, step, 0)
 
+    def later(w, visit):
+        def step(i, carry):
+            visit(Y - 1 - i if w == 0 else i)
+            return carry
+
+        lax.fori_loop(0, Y - 1 - y if w == 0 else y, step, 0)
+
     def z_device(other):
         return (y * Z + other, mine)
 
@@ -136,6 +167,8 @@
     def greet(device):
         pl.semaphore_signal(barrier, inc=1, device_id=device, device_id_type=MESH)
 
+    for load in loads:
+        load.start()
     across(lambda other: greet(z_device(other)))
     peers(Y, y, lambda other: greet(y_device(other)))
     peers(N, mine, lambda other: greet(x_device(other)))
@@ -145,6 +178,8 @@
     causal = t_i >= s_i
     eye = t_i == s_i
     lower = causal.astype(F32)
+    for load in loads[:3]:
+        load.wait()
     ld = ld_ref[...]
     cum_row = dot(ld, lower, NT, lax.Precision.HIGHEST)
     cum_col = dot(lower, ld, NT, lax.Precision.HIGHEST)
@@ -248,7 +283,7 @@
             both_s[w, c] = jnp.exp(trail_t) * lead + trail
             across(lambda other: in_copy(w, c, other, m).start())
 
-    def scan(w):
+    def scan(w, use):
         for c in range(C):
             if w == 0 and c == 0:
                 across(lambda other: two_copy(other, half_of(other)).wait_recv())
@@ -268,17 +303,18 @@
             )
             row_out[w, c, 0:part, :] = total
             row_out[w, c, part : part + 8, :] = jnp.broadcast_to(passed, (8, D))
-            peers(Y, y, lambda other: y_copy(w, c, other, y).start())
+            later(w, lambda other: y_copy(w, c, other, y).start())
         for c in range(C):
-            peers(Y, y, lambda other: y_copy(w, c, other, other).wait_recv())
-            row_in[w, c, y] = row_out[w, c]
-            before = jnp.zeros((part, D), F32)
-            for i in range(Y):
+
+            def gain(i, before):
                 at = i if w == 0 else Y - 1 - i
+                y_copy(w, c, at, at).wait_recv()
                 grown = jnp.exp(row_in[w, c, at, part : part + 1, :]) * before
-                grown = grown + row_in[w, c, at, 0:part, :]
-                use = y > at if w == 0 else y < at
-                before = jnp.where(use, grown, before)
+                return grown + row_in[w, c, at, 0:part, :]
+
+            before = lax.fori_loop(
+                0, y if w == 0 else Y - 1 - y, gain, jnp.zeros((part, D), F32)
+            )
 
             def leave(other):
                 at = half_of(other)
@@ -308,6 +344,8 @@
             across(land, near_first=True)
         for c in range(C):
             across(lambda other: forward_copy(w, c, 1 - b, half_of(other)).wait_recv())
+            for h in (c, C + c):
+                use(h)
 
     totals = [jnp.broadcast_to(totals[h : h + 1, :], (1, D)) for h in range(H)]
     for h in range(H):
@@ -331,6 +369,8 @@
     across(lambda other: two_copy(other, m).start())
     enter(0)
 
+    for load in loads[3:]:
+        load.wait()
     for h in range(H):
         column = jnp.broadcast_to(cum_col[:, h : h + 1], (T, T))
         growth = jnp.exp(column)
@@ -346,11 +386,10 @@
         sqt_s[h, :, 0:T] = high
         sqt_s[h, :, T : 2 * T] = low
 
-    scan(0)
-
-    squares = jnp.zeros((T, D), F32)
-    inner = jnp.zeros((T, D), F32)
-    for h in range(H):
+    squares = []
+    inner = []
+
+    def output(h):
         high, low = halves(state[0, h * D : (h + 1) * D, :])
         q_one = head(q_ref, h)
         carried = dot(
@@ -358,8 +397,10 @@
         )
         raw = growth_s[h] * carried + intra_s[h]
         raw_s[h] = raw
-        squares = squares + raw * raw
-        inner = inner + raw * head(ct_ref, h).astype(F32)
+        squares.append(raw * raw)
+        inner.append(raw * head(ct_ref, h).astype(F32))
+
+    scan(0, output)
 
     def to_row(x):
         column = jnp.sum(x, axis=1, keepdims=True)
@@ -368,8 +409,8 @@
     def to_column(x):
         return jnp.sum(jnp.where(eye, x, 0.0), axis=1, keepdims=True)
 
-    sums_out[0:1, :] = to_row(squares)
-    sums_out[1:2, :] = to_row(inner)
+    sums_out[0:1, :] = to_row(sum(squares[1:], squares[0]))
+    sums_out[1:2, :] = to_row(sum(inner[1:], inner[0]))
     peers(N, mine, lambda other: x_copy(other, mine).start())
     sums_in[mine] = sums_out[...]
     peers(N, mine, lambda other: x_copy(other, other).wait_recv())
@@ -407,9 +448,14 @@
         raw_s[h] = dot(grad_weights, head(q_ref, h), TN)
         intra_s[h] = dot(weights_s[h], grad, TN)
 
-    scan(1)
-
-    for h in range(H):
+    saves = [
+        pltpu.make_async_copy(att_ref, att_hbm, save_sem.at[0]),
+        pltpu.make_async_copy(qg_ref, qg_hbm, save_sem.at[1]),
+    ]
+    for save in saves:
+        save.start()
+
+    def gradients(h):
         columns = slice(h * D, (h + 1) * D)
         high, low = halves(state[1, h * D : (h + 1) * D, :])
         v_one = head(v_ref, h)
@@ -422,6 +468,14 @@
         )
         kg_ref[:, columns] = (raw_s[h] + fade_s[h] * key_part).astype(BF16)
         vg_ref[:, columns] = (intra_s[h] + fade_s[h] * value_part).astype(BF16)
+        for i, (src, dst) in enumerate(((kg_ref, kg_hbm), (vg_ref, vg_hbm))):
+            save = pltpu.make_async_copy(
+                src.at[:, columns], dst.at[:, columns], grad_sem.at[i, h]
+            )
+            save.start()
+            saves.append(save)
+
+    scan(1, gradients)
 
     t_copy().wait_send()
     across(lambda other: two_copy(other, m).wait_send())
@@ -429,17 +483,32 @@
         for c in range(C):
             pair_copy(w, c).wait_send()
             across(lambda other: in_copy(w, c, other, m).wait_send())
-            peers(Y, y, lambda other: y_copy(w, c, other, y).wait_send())
+            later(w, lambda other: y_copy(w, c, other, y).wait_send())
             across(lambda other: out_copy(w, c, other, m).wait_send())
             across(lambda other: forward_copy(w, c, b, half_of(other)).wait_send())
     peers(N, mine, lambda other: x_copy(other, mine).wait_send())
-
-
-def hand_over(a_ref, b_ref, c_ref, d_ref, a_out, b_out, c_out, d_out):
-    a_out[...] = a_ref[...]
-    b_out[...] = b_ref[...]
-    c_out[...] = c_ref[...]
-    d_out[...] = d_ref[...]
+    for save in saves:
+        save.wait()
+
+
+def hand_over(*refs):
+    sources, targets, held = refs[0:4], refs[4:8], refs[8:12]
+    load_sem, save_sem = refs[12:14]
+    loads = [
+        pltpu.make_async_copy(src, dst, load_sem.at[i])
+        for i, (src, dst) in enumerate(zip(sources, held))
+    ]
+    saves = [
+        pltpu.make_async_copy(src, dst, save_sem.at[i])
+        for i, (src, dst) in enumerate(zip(held, targets))
+    ]
+    for load in loads:
+        load.start()
+    for load, save in zip(loads, saves):
+        load.wait()
+        save.start()
+    for save in saves:
+        save.wait()
 
 
 def local(query_rows, key_rows, value_rows, log_decay, cotangent):
@@ -453,15 +522,27 @@
     M = Z // 2
     size = H * D // (2 * C)
     part = size // M
-    vmem = pl.BlockSpec(memory_space=pltpu.VMEM)
+    anywhere = pl.BlockSpec(memory_space=pl.ANY)
     dma = pltpu.SemaphoreType.DMA
     out = jax.ShapeDtypeStruct(query_rows.shape, BF16)
     results = pl.pallas_call(
         functools.partial(kernel, Y, Z, N, C),
         out_shape=(out,) * 4,
-        in_specs=[vmem] * 5,
-        out_specs=(vmem,) * 4,
+        in_specs=[anywhere] * 5,
+        out_specs=(anywhere,) * 4,
         scratch_shapes=[
+            pltpu.VMEM((T, H * D), BF16),
+            pltpu.VMEM((T, H * D), BF16),
+            pltpu.VMEM((T, H * D), BF16),
+            pltpu.VMEM((H, T), F32),
+            pltpu.VMEM((T, H * D), BF16),
+            pltpu.VMEM((T, H * D), BF16),
+            pltpu.VMEM((T, H * D), BF16),
+            pltpu.VMEM((T, H * D), BF16),
+            pltpu.VMEM((T, H * D), BF16),
+            dma((5,)),
+            dma((2,)),
+            dma((2, H)),
             pltpu.VMEM((2, H * D, D), F32),
             pltpu.VMEM((2, C, size, D), F32),
             pltpu.VMEM((2, C, size, D), F32),
@@ -509,8 +590,9 @@
     return pl.pallas_call(
         hand_over,
         out_shape=(out,) * 4,
-        in_specs=[vmem] * 4,
-        out_specs=(vmem,) * 4,
+        in_specs=[anywhere] * 4,
+        out_specs=(anywhere,) * 4,
+        scratch_shapes=[pltpu.VMEM((T, H * D), BF16)] * 4 + [dma((4,)), dma((4,))],
     )(*results)
 
 

time: 93.6 us -> 91.1 us (0.973)
  the two profiles are of different devices: /device:TPU:2 before, /device:TPU:64 now
where the time goes in v3:
time: 91.1 us; the launch traced here: 90.9 us
  Pallas kernels  90.3 us (99%)
    pallas_call x1, Pallas kernels, local(): pl.pallas_call(functools.partial(kernel, Y, Z, N, C), out_shape=(out,) *...  88.5 us

profile of v3, /device:TPU:64, one launch (start us, length us, event | category | flops | bytes accessed | tf_op | source)
XLA Modules:
  0.0 90.9 jit_solution(15367816293533739763)
XLA Ops:
  0.6 88.5 %shard_map.84 = (bf16[128,512]{1,0:T(8,128)(2,1)}, bf16[128,512]{1,0:T(8,128)(2,1)}, bf16[128,512]{1,0:T(8,128)(2,1)}, bf16[128,512]{1,0:T(8,128)(2,1)}) custom-call(bf16[128,512]{1,0:T(8,128)(2,1)} %q_hbm.1, bf16[128,512]{1,0:T(8,128)(2,1)} %k_hbm.1, bf16[128,512]{1,0:T(8,128)(2,1)} %v_hbm.1, f32[4,128]{1,0:T(4,128)} %ld_hbm.1, bf16[128,512]{1,0:T(8,128)(2,1)} %ct_hbm.1), custom_call_target="tpu_custom_call" | custom-call | tf_op jit(solution)/shard_map/pallas_call | solution.py:528
  89.1 1.8 %shard_map.85 = (bf16[128,512]{1,0:T(8,128)(2,1)}, bf16[128,512]{1,0:T(8,128)(2,1)}, bf16[128,512]{1,0:T(8,128)(2,1)}, bf16[128,512]{1,0:T(8,128)(2,1)}) custom-call(bf16[128,512]{1,0:T(8,128)(2,1)} %get-tuple-element.8.refs_0_, bf16[128,512]{1,0:T(8,128)(2,1)} %get-tuple-element.9.refs_1_, bf16[128,512]{1,0:T(8,128)(2,1)} %get-tuple-element.10.refs_2_, ...), custom_call_target="tpu_custom_call" | custom-call | tf_op jit(solution)/shard_map/pallas_call | solution.py:590
